TPU v7x, 32 devices: a whole 2x2x4 slice. The times are simulated.
32 devices in a mesh: dp: 8 (over z, x), mp: 4 (over y, core).
Axes of the slice: x: 2, y: 2, z: 4, core: 2. Of those that a mesh axis runs over, the one named last changes fastest.
Arguments:
- tokens: bfloat16 [32768, 768], P('dp'), may hold values from -6 to 6
- segment: int32 [32768], P('dp'), may hold values from 0 to 8, as said below
- ln1_gain: bfloat16 [768], P('mp'), may hold values from 0.5 to 1.5
- ln1_bias: bfloat16 [768], P('mp'), may hold values from -2 to 2
- w_qkv: bfloat16 [3, 768, 768], P(None, None, 'mp'), may hold values from -0.21875 to 0.21875
- b_qv: bfloat16 [2, 768], P(None, 'mp'), may hold values from -2 to 2
- w_out: bfloat16 [768, 768], P('mp'), may hold values from -0.875 to 0.875
- b_out: bfloat16 [768], P('mp'), may hold values from -2 to 2
- ln2_gain: bfloat16 [768], P('mp'), may hold values from 0.5 to 1.5
- ln2_bias: bfloat16 [768], P('mp'), may hold values from -2 to 2
- w_up: bfloat16 [768, 3072], P(None, 'mp'), may hold values from -0.21875 to 0.21875
- b_up: bfloat16 [3072], P('mp'), may hold values from -3 to 3
- w_down: bfloat16 [3072, 768], P('mp'), may hold values from -0.109375 to 0.109375
- b_down: bfloat16 [768], P('mp'), may hold values from -2 to 2
- cotangent: bfloat16 [32768, 768], P(('dp', 'mp')), may hold values from -6 to 6
Outputs:
- output: bfloat16 [32768, 768], P(('dp', 'mp'))
- grad_x: float32 [32768, 768], P(('dp', 'mp'))
- grad_ln1_gain: float32 [768], P('mp')
- grad_ln1_bias: float32 [768], P('mp')
- grad_w_qkv: float32 [3, 768, 768], P(None, None, 'mp')
- grad_b_qv: float32 [2, 768], P(None, 'mp')
- grad_w_out: float32 [768, 768], P('mp')
- grad_b_out: float32 [768], P('mp')
- grad_ln2_gain: float32 [768], P('mp')
- grad_ln2_bias: float32 [768], P('mp')
- grad_w_up: float32 [768, 3072], P(None, 'mp')
- grad_b_up: float32 [3072], P('mp')
- grad_w_down: float32 [3072, 768], P('mp')
- grad_b_down: float32 [768], P('mp')
Inputs may be any that keep to these rules, and one draw needn't show every extreme that they name: `segment`: within each aligned sequence of 512 rows the numbers never fall except to 0; 0 marks padding rows, which stand at the end of a sequence.
All inputs are finite; a program needn't handle non-finite values.
Results may differ from a plain program's by a relative error of at most 0.018.
Values may be sent and summed in bfloat16 or wider, within the bound.
A program may use at most 256 MiB of HBM per device.

v0:
```python
import jax
import jax.numpy as jnp
from jax import lax
from jax.sharding import PartitionSpec as P

HD = 64
LEN = 512


def layer_norm(values, norm_gain, norm_shift):
    centered = values - jnp.mean(values, axis=-1, keepdims=True)
    spread = jnp.mean(centered * centered, axis=-1, keepdims=True)
    return centered * lax.rsqrt(spread + 1e-06) * norm_gain + norm_shift


def norm_back(values, norm_gain, norm_shift, incoming):
    result, pull_back = jax.vjp(layer_norm, values, norm_gain, norm_shift)
    return pull_back(incoming)


def gelu_exact(values):
    return jax.nn.gelu(values, approximate=False)


def gelu_back(values, incoming):
    result, pull_back = jax.vjp(gelu_exact, values)
    return pull_back(incoming)[0]


def plain_dot(left, right):
    return jnp.dot(left, right, preferred_element_type=jnp.float32)


def over_rows(left, right):
    return lax.dot_general(
        left, right, (((0,), (0,)), ((), ())), preferred_element_type=jnp.float32
    )


def against(left, right):
    return lax.dot_general(
        left, right, (((1,), (1,)), ((), ())), preferred_element_type=jnp.float32
    )


def allowed_pairs(segment):
    length = segment.shape[0]
    row_ids = lax.broadcasted_iota(jnp.int32, (length, length), 0)
    col_ids = lax.broadcasted_iota(jnp.int32, (length, length), 1)
    same = (segment[:, None] == segment[None, :]) & (segment[None, :] != 0)
    return same | (row_ids == col_ids)


def head_scores(query_heads, key_heads, segment):
    score_scale = query_heads.shape[-1] ** (-0.5)
    scores = (
        jnp.einsum("qhd,khd->hqk", query_heads, key_heads, preferred_element_type=jnp.float32)
        * score_scale
    )
    return jnp.where(allowed_pairs(segment)[None], scores, -1e30)


def attend_forward(entries):
    query_heads, key_heads, value_heads, segment = entries
    masked = head_scores(query_heads, key_heads, segment)
    row_max = jnp.max(masked, axis=-1, keepdims=True)
    expo_scores = jnp.exp(masked - row_max)
    row_sum = jnp.sum(expo_scores, axis=-1, keepdims=True)
    attn_probs = (expo_scores / row_sum).astype(jnp.bfloat16)
    attended = jnp.einsum(
        "hqk,khd->qhd", attn_probs, value_heads, preferred_element_type=jnp.float32
    )
    return (attended.astype(jnp.bfloat16), (row_max + jnp.log(row_sum))[..., 0])


def attend_backward(entries):
    query_heads, key_heads, value_heads, segment, log_total, grad_heads = entries
    score_scale = query_heads.shape[-1] ** (-0.5)
    attn_probs = jnp.exp(head_scores(query_heads, key_heads, segment) - log_total[..., None])
    grad_probs = jnp.einsum(
        "qhd,khd->hqk", grad_heads, value_heads, preferred_element_type=jnp.float32
    )
    inner = jnp.sum(attn_probs * grad_probs, axis=-1, keepdims=True)
    grad_scores = (attn_probs * (grad_probs - inner)).astype(jnp.bfloat16)
    grad_query = (
        jnp.einsum("hqk,khd->qhd", grad_scores, key_heads, preferred_element_type=jnp.float32)
        * score_scale
    )
    grad_key = (
        jnp.einsum("hqk,qhd->khd", grad_scores, query_heads, preferred_element_type=jnp.float32)
        * score_scale
    )
    grad_value = jnp.einsum(
        "hqk,qhd->khd",
        attn_probs.astype(jnp.bfloat16),
        grad_heads,
        preferred_element_type=jnp.float32,
    )
    return (
        grad_query.astype(jnp.bfloat16),
        grad_key.astype(jnp.bfloat16),
        grad_value.astype(jnp.bfloat16),
    )


def per_device(
    tokens,
    segment,
    ln1_gain,
    ln1_bias,
    w_qkv,
    b_qv,
    w_out,
    b_out,
    ln2_gain,
    ln2_bias,
    w_up,
    b_up,
    w_down,
    b_down,
    cotangent,
):
    group_rows = tokens.shape[0]
    group_size = lax.axis_size("mp")
    my_index = lax.axis_index("mp")
    row_count = group_rows // group_size
    sequences = group_rows // LEN
    heads_here = w_qkv.shape[2] // HD
    (
        gain_one,
        shift_one,
        gain_two,
        shift_two,
        bias_out,
        bias_down,
        bias_up,
        full_out,
        full_up,
        full_down,
    ) = (
        lax.all_gather(ln1_gain, "mp", axis=0, tiled=True),
        lax.all_gather(ln1_bias, "mp", axis=0, tiled=True),
        lax.all_gather(ln2_gain, "mp", axis=0, tiled=True),
        lax.all_gather(ln2_bias, "mp", axis=0, tiled=True),
        lax.all_gather(b_out, "mp", axis=0, tiled=True),
        lax.all_gather(b_down, "mp", axis=0, tiled=True),
        lax.all_gather(b_up, "mp", axis=0, tiled=True),
        lax.all_gather(w_out, "mp", axis=0, tiled=True),
        lax.all_gather(w_up, "mp", axis=1, tiled=True),
        lax.all_gather(w_down, "mp", axis=0, tiled=True),
    )
    gain_one = gain_one.astype(jnp.float32)
    shift_one = shift_one.astype(jnp.float32)
    gain_two = gain_two.astype(jnp.float32)
    shift_two = shift_two.astype(jnp.float32)
    tokens_wide = tokens.astype(jnp.float32)
    normed = layer_norm(tokens_wide, gain_one, shift_one).astype(jnp.bfloat16)
    query = (plain_dot(normed, w_qkv[0]) + b_qv[0].astype(jnp.float32)).astype(jnp.bfloat16)
    key_rows = plain_dot(normed, w_qkv[1]).astype(jnp.bfloat16)
    value_rows = (plain_dot(normed, w_qkv[2]) + b_qv[1].astype(jnp.float32)).astype(jnp.bfloat16)
    shaped = (sequences, LEN, heads_here, HD)
    query_seq = query.reshape(shaped)
    key_seq = key_rows.reshape(shaped)
    value_seq = value_rows.reshape(shaped)
    segment_seq = segment.reshape(sequences, LEN)
    attended, log_total = lax.map(attend_forward, (query_seq, key_seq, value_seq, segment_seq))
    attended = attended.reshape(group_rows, heads_here * HD)
    my_rows = lax.dynamic_slice_in_dim(tokens_wide, my_index * row_count, row_count, 0)
    attended_rows = lax.all_to_all(attended, "mp", split_axis=0, concat_axis=1, tiled=True)
    projected = plain_dot(attended_rows, full_out)
    hidden = my_rows + projected + bias_out.astype(jnp.float32)
    normed_two = layer_norm(hidden, gain_two, shift_two).astype(jnp.bfloat16)
    cot_wide = cotangent.astype(jnp.float32)
    up_proj = plain_dot(normed_two, full_up) + bias_up.astype(jnp.float32)
    active = gelu_exact(up_proj).astype(jnp.bfloat16)
    output = hidden + plain_dot(active, full_down) + bias_down.astype(jnp.float32)
    grad_up = gelu_back(up_proj, against(cotangent, full_down)).astype(jnp.bfloat16)
    grad_down = over_rows(active, cotangent)
    grad_upw = over_rows(normed_two, grad_up)
    grad_bias_up = jnp.sum(grad_up.astype(jnp.float32), axis=0)
    grad_normed_two = against(grad_up, full_up)
    grad_bias_down = jnp.sum(cot_wide, axis=0)
    grad_hidden_norm, grad_gain_two, grad_shift_two = norm_back(
        hidden, gain_two, shift_two, grad_normed_two
    )
    grad_hidden = cot_wide + grad_hidden_norm
    grad_bias_out = jnp.sum(grad_hidden, axis=0)
    grad_proj = grad_hidden.astype(jnp.bfloat16)
    grad_outw = over_rows(attended_rows, grad_proj)
    grad_attended = lax.all_to_all(
        against(grad_proj, full_out).astype(jnp.bfloat16),
        "mp",
        split_axis=1,
        concat_axis=0,
        tiled=True,
    )
    grad_query, grad_key, grad_value = lax.map(
        attend_backward,
        (query_seq, key_seq, value_seq, segment_seq, log_total, grad_attended.reshape(shaped)),
    )
    grad_query = grad_query.reshape(group_rows, heads_here * HD)
    grad_key = grad_key.reshape(group_rows, heads_here * HD)
    grad_value = grad_value.reshape(group_rows, heads_here * HD)
    grad_qkvw = jnp.stack(
        [over_rows(normed, grad_query), over_rows(normed, grad_key), over_rows(normed, grad_value)]
    )
    grad_bias_qv = jnp.stack(
        [
            jnp.sum(grad_query.astype(jnp.float32), axis=0),
            jnp.sum(grad_value.astype(jnp.float32), axis=0),
        ]
    )
    partial_normed = (
        against(grad_query, w_qkv[0]) + against(grad_key, w_qkv[1]) + against(grad_value, w_qkv[2])
    )
    grad_normed = lax.psum_scatter(
        partial_normed.astype(jnp.bfloat16), "mp", scatter_dimension=0, tiled=True
    ).astype(jnp.float32)
    grad_input_norm, grad_gain_one, grad_shift_one = norm_back(
        my_rows, gain_one, shift_one, grad_normed
    )
    grad_input = grad_hidden + grad_input_norm
    (
        share_gain_one,
        share_shift_one,
        share_gain_two,
        share_shift_two,
        share_bias_out,
        share_bias_down,
        share_bias_up,
        share_outw,
        share_upw,
        share_down,
    ) = (
        lax.psum_scatter(
            grad_gain_one.astype(jnp.bfloat16), "mp", scatter_dimension=0, tiled=True
        ).astype(jnp.float32),
        lax.psum_scatter(
            grad_shift_one.astype(jnp.bfloat16), "mp", scatter_dimension=0, tiled=True
        ).astype(jnp.float32),
        lax.psum_scatter(
            grad_gain_two.astype(jnp.bfloat16), "mp", scatter_dimension=0, tiled=True
        ).astype(jnp.float32),
        lax.psum_scatter(
            grad_shift_two.astype(jnp.bfloat16), "mp", scatter_dimension=0, tiled=True
        ).astype(jnp.float32),
        lax.psum_scatter(
            grad_bias_out.astype(jnp.bfloat16), "mp", scatter_dimension=0, tiled=True
        ).astype(jnp.float32),
        lax.psum_scatter(
            grad_bias_down.astype(jnp.bfloat16), "mp", scatter_dimension=0, tiled=True
        ).astype(jnp.float32),
        lax.psum_scatter(
            grad_bias_up.astype(jnp.bfloat16), "mp", scatter_dimension=0, tiled=True
        ).astype(jnp.float32),
        lax.psum_scatter(
            grad_outw.astype(jnp.bfloat16), "mp", scatter_dimension=0, tiled=True
        ).astype(jnp.float32),
        lax.psum_scatter(
            grad_upw.astype(jnp.bfloat16), "mp", scatter_dimension=1, tiled=True
        ).astype(jnp.float32),
        lax.psum_scatter(
            grad_down.astype(jnp.bfloat16), "mp", scatter_dimension=0, tiled=True
        ).astype(jnp.float32),
    )
    summed = lax.psum(
        (
            share_gain_one,
            share_shift_one,
            grad_qkvw,
            grad_bias_qv,
            share_outw,
            share_bias_out,
            share_gain_two,
            share_shift_two,
            share_upw,
            share_bias_up,
            share_down,
            share_bias_down,
        ),
        "dp",
    )
    return (
        output.astype(jnp.bfloat16),
        grad_input,
        summed[0],
        summed[1],
        summed[2],
        summed[3],
        summed[4],
        summed[5],
        summed[6],
        summed[7],
        summed[8],
        summed[9],
        summed[10],
        summed[11],
    )


def solution(mesh):
    placed = (
        P("dp", None),
        P("dp"),
        P("mp"),
        P("mp"),
        P(None, None, "mp"),
        P(None, "mp"),
        P("mp", None),
        P("mp"),
        P("mp"),
        P("mp"),
        P(None, "mp"),
        P("mp"),
        P("mp", None),
        P("mp"),
        P(("dp", "mp"), None),
    )
    return jax.shard_map(
        per_device,
        mesh=mesh,
        in_specs=placed,
        out_specs=(
            P(("dp", "mp"), None),
            P(("dp", "mp"), None),
            P("mp"),
            P("mp"),
            P(None, None, "mp"),
            P(None, "mp"),
            P("mp", None),
            P("mp"),
            P("mp"),
            P("mp"),
            P(None, "mp"),
            P("mp"),
            P("mp", None),
            P("mp"),
        ),
        check_vma=False,
    )
```

profile of v0, /device:TPU:0, one launch (start us, length us, event | category | flops | bytes accessed | tf_op | source)
XLA Modules:
  0.0 748.0 jit_solution(18345992957422097749)
XLA Ops:
  14.9 13.4 %all-reduce.15 = (bf16[768]{0:T(1024)(128)(2,1)S(1)}, bf16[768]{0:T(1024)(128)(2,1)S(1)}, bf16[768]{0:T(1024)(128)(2,1)S(1)}, bf16[768]{0:T(1024)(128)(2,1)S(1)}, bf16[768]{0:T(1024)(128)(2,1)S(1)}) all-reduce(bf16[768]{0:T(1024)(128)(2,1)S(1)} %dynamic-update-slice.1, ...), channel_id=1, replica_groups=mesh['dp'=8,'mp'=4] {'mp'}, use_global_device_ids=true, to_apply=%add.1 | all-reduce | flops 3840 | bytes 15360
  28.3 8.6 %copy.80 = bf16[4096,768]{0,1:T(8,128)(2,1)} copy(bf16[4096,768]{1,0:T(8,128)(2,1)} %param.19) | data formatting | bytes 12582912 | tf_op args[0]
  36.9 4.7 convert_reduce_fusion
  44.7 3.5 add_convert_fusion.2
  58.4 40.7 %while.26 = (s32[]{:T(128)}, bf16[8,512,3,64]{1,3,2,0:T(8,128)(2,1)}, f32[8,3,512]{2,1,0:T(4,128)}, bf16[8,512,3,64]{1,3,2,0:T(8,128)(2,1)}, s32[8,512]{1,0:T(8,...) while((s32[]{:T(128)}, ...), condition=%wide.region_5.6_spmd, body=%wide.region_2.5_spmd.sunk | while | flops 211909632 | bytes 11333209 | solution.py:166
  61.0 2.7 fusion.146
  66.0 2.7 fusion.146
  71.1 2.7 fusion.146
  76.2 2.7 fusion.146
  81.3 2.7 fusion.146
  86.3 2.7 fusion.146
  91.4 2.7 fusion.146
  96.5 2.7 fusion.146
  99.2 4.6 copy.84
  103.7 3.7 all_to_all.26
  107.5 3.0 copy.85
  110.5 3.6 all-to-all-start
  114.9 9.2 %convert_element_type.163 = f32[4096,768]{0,1:T(8,128)} convert(bf16[4096,768]{0,1:T(8,128)(2,1)} %copy.80) | non-fusion elementwise | flops 3145728 | bytes 18874368 | tf_op jit(solution)/shard_map/convert_element_type | solution.py:156
  124.1 16.9 %all-gather = bf16[4,1,768]{2,1,0:T(2,128)(2,1)S(1)} all-gather(bf16[1,1,768]{2,1,0:T(2,128)(2,1)S(1)} %reshape.310), channel_id=1, replica_groups=mesh['dp'=8,'mp'=4] {'mp'}, dimensions={0}, use_global_device_ids=true | all-gather | bytes 7680 | tf_op jit(solution)/shard_map/all_gather | solution.py:147
  143.8 4.3 fusion.91
  148.5 37.7 %multiply_convert_fusion.1 = (bf16[1024,3072]{1,0:T(8,128)(2,1)}, f32[1024,3072]{1,0:T(8,128)}, f32[1024,3072]{1,0:T(8,128)}) fusion(f32[3072]{0:T(1024)S(1)} %bitcast.224, bf16[768,3072]{1,0:T(8,128)(2,1)} %all-gather.7.cloned.1.call-done, f32[1024,768]{0,1:T(8,128)S(1)} %get-tuple-element.289, f32[768]{0:T(1024)S(1)} %convert_element_type.172, ...), kind=kOutput, calls=%fused_computation.70 | convolution fusion | flops 5043388416 | bytes 39348224 | tf_op jit(solution)/shard_map/dot_general | solution.py:31
  186.2 18.7 %fusion.93 = (bf16[3072]{0:T(1024)(128)(2,1)S(1)}, bf16[1024,3072]{1,0:T(8,128)(2,1)}) fusion(f32[1024,3072]{1,0:T(8,128)} %get-tuple-element.275, bf16[1024,768]{1,0:T(8,128)(2,1)} %param.33, bf16[3072,768]{1,0:T(8,128)(2,1)} %all-gather.9.cloned.1.call-done, f32[1024,3072]{1,0:T(8,128)} %get-tuple-element.290, f32[3072]{0:T(1024)S(1)} %bitcast.225), kind=kOutput, calls=%fused_computation.165 | convolution fusion | flops 4882166784 | bytes 37767168 | tf_op jit(solution)/shard_map/dot_general | solution.py:41
  204.9 9.8 %fusion.92 = (bf16[768]{0:T(1024)(128)(2,1)S(1)}, f32[1024,768]{1,0:T(8,128)}) fusion(bf16[1024,3072]{1,0:T(8,128)(2,1)} %get-tuple-element.294, bf16[768,3072]{1,0:T(8,128)(2,1)} %all-gather.7.cloned.1.call-done), kind=kOutput, calls=%fused_computation.164 | convolution fusion | flops 4832623616 | bytes 14157312 | tf_op jit(solution)/shard_map/dot_general | solution.py:41
  214.7 3.6 copy.88
  218.2 2.9 multiply_reduce_fusion.2
  224.9 2.5 convolution_convert_fusion.4
  227.4 9.9 %convolution_convert_fusion.1 = bf16[768,3072]{1,0:T(8,128)(2,1)} fusion(bf16[1024,3072]{1,0:T(8,128)(2,1)} %get-tuple-element.294, f32[1024,768]{0,1:T(8,128)S(1)} %get-tuple-element.289, f32[768]{0:T(1024)S(1)} %convert_element_type.172, f32[768]{0:T(1024)S(1)} %convert_element_type.171, f32[1024]{0:T(1024)S(1)} %fusion.85, ...), kind=kOutput, calls=%fused_computation.88 | convolution fusion | flops 4838129664 | bytes 14170112 | tf_op jit(solution)/shard_map/dot_general | solution.py:35
  237.3 4.3 convolution_convert_fusion.3
  241.6 4.4 all-to-all-start.1
  246.1 9.1 %convolution_convert_fusion = bf16[3072,768]{1,0:T(8,128)(2,1)} fusion(bf16[1024,3072]{1,0:T(8,128)(2,1)} %get-tuple-element.274, bf16[1024,768]{1,0:T(8,128)(2,1)} %param.33), kind=kOutput, calls=%fused_computation.87 | convolution fusion | flops 4834197504 | bytes 12582912 | tf_op jit(solution)/shard_map/dot_general | solution.py:35
  255.3 14.3 %all-to-all-done.1 = bf16[1024,4,192]{0,2,1:T(8,128)(2,1)} async-done(((bf16[1024,4,192]{0,2,1:T(8,128)(2,1)}), bf16[1024,4,192]{0,2,1:T(8,128)(2,1)}, u32[]{:S(2)}, u32[]{:S(2)}) %all-to-all-start.1) | async-done | bytes 1572896 | tf_op jit(solution)/shard_map/all_to_all | solution.py:190
  269.6 3.9 copy.89
  273.4 3.5 reshape.286
  276.9 3.2 copy.92
  284.1 102.6 %while.27 = (s32[]{:T(128)}, bf16[8,512,3,64]{1,3,2,0:T(8,128)(2,1)}, bf16[8,512,3,64]{1,3,2,0:T(8,128)(2,1)}, bf16[8,512,3,64]{1,3,2,0:T(8,128)(2,1)}, bf16[8,5...) while((s32[]{:T(128)}, ...), condition=%wide.region_12.13_spmd, body=%wide.region_10.12_spmd.sunk | while | flops 511933440 | bytes 26126452 | solution.py:197
  290.5 2.2 fusion.158
  303.3 2.2 fusion.158
  316.1 2.2 fusion.158
  320.3 2.2 fusion.159
  328.9 2.3 fusion.158
  333.2 2.2 fusion.159
  341.8 2.2 fusion.158
  354.6 2.2 fusion.158
  358.8 2.2 fusion.159
  367.4 2.2 fusion.158
  380.1 2.2 fusion.158
  386.7 2.4 copy.98
  393.4 6.4 fusion.71
  399.8 6.3 fusion.74
  406.1 12.1 %add_convert_fusion = bf16[4096,768]{0,1:T(8,128)(2,1)} fusion(f32[4096,768]{0,1:T(8,128)} %fusion.74, f32[4096,768]{0,1:T(8,128)} %fusion.71, bf16[4096,192]{0,1:T(8,128)(2,1)S(1)} %bitcast.206, bf16[3,768,192]{1,2,0:T(8,128)(2,1)S(1)} %copy-done.24), kind=kOutput, calls=%fused_computation.68 | convolution fusion | flops 1217396736 | bytes 33325056 | tf_op jit(solution)/shard_map/dot_general | solution.py:41
  422.0 2.5 dynamic-slice_reduce_fusion
  427.1 6.8 convolution_bitcast_fusion
  434.0 5.2 convolution_bitcast_fusion.1
  439.2 2.2 convolution_bitcast_fusion.2
  442.9 33.4 %reduce-scatter.5.cloned.1.call-done = bf16[1024,768]{0,1:T(8,128)(2,1)} async-done(((bf16[4096,768]{0,1:T(8,128)(2,1)}), bf16[1024,768]{0,1:T(8,128)(2,1)}) %reduce-scatter.5.cloned.1.call-update) | async-done | bytes 1572880 | tf_op jit(solution)/shard_map/reduce_scatter | solution.py:216
  476.3 3.2 multiply_reduce_fusion.3
  479.6 3.6 fusion.67
  483.2 5.3 add_add_fusion.2
  490.2 11.2 %all-reduce.14 = (bf16[768]{0:T(1024)(128)(2,1)S(1)}, bf16[768]{0:T(1024)(128)(2,1)S(1)}, bf16[768]{0:T(1024)(128)(2,1)S(1)}, bf16[768]{0:T(1024)(128)(2,1)S(1)}...) all-reduce(bf16[768]{0:T(1024)(128)(2,1)S(1)} %dynamic-update-slice, ...), channel_id=1, replica_groups=mesh['dp'=8,'mp'=4] {'mp'}, use_global_device_ids=true, to_apply=%add.5 | all-reduce | flops 8448 | bytes 33792
  501.4 9.5 %add_convert_fusion.3 = bf16[1024,768]{0,1:T(8,128)(2,1)} fusion(f32[1024,768]{0,1:T(8,128)S(1)} %get-tuple-element.289, bf16[1024,3072]{1,0:T(8,128)(2,1)} %get-tuple-element.274, bf16[3072,768]{1,0:T(8,128)(2,1)} %all-gather.9.cloned.1.call-done, f32[768]{0:T(1024)S(1)} %convert_element_type.176), kind=kOutput, calls=%fused_computation.109 | convolution fusion | flops 4834197504 | bytes 15731712 | tf_op jit(solution)/shard_map/dot_general | solution.py:31
  511.0 2.7 copy.101
  513.7 2.4 copy.102
  516.4 221.8 %all-reduce.20 = (f32[192]{0:T(256)}, f32[192]{0:T(256)}, f32[2,192]{1,0:T(2,128)}, f32[192,768]{1,0:T(8,128)}, f32[192]{0:T(256)}, /*index=5*/f32[192]{0:T(256)...) all-reduce(f32[192]{0:T(256)S(1)} %get-tuple-element.302, ...), channel_id=1, replica_groups=mesh['dp'=8,'mp'=4] {'dp'}, use_global_device_ids=true, to_apply=%region_20.21 | all-reduce | flops 1329408 | bytes 7981056 | tf_op jit(solution)/shard_map/psum | solution.py:266
  738.1 2.8 copy.168
  (263 shorter events, 141.5 us)
Async XLA Ops:
  7.2 135.5 %all-gather.5.cloned.1.call-start = ((), (), s32[]{:S(2)}) async-start(), calls=%async_computation.6 | async-start | bytes 1474560 | tf_op jit(solution)/shard_map/all_gather | solution.py:148
  7.9 140.6 %all-gather.7.cloned.1.call-start = ((), (), s32[]{:S(2)}) async-start(), calls=%async_computation.7 | async-start | bytes 5898240 | tf_op jit(solution)/shard_map/all_gather | solution.py:149
  28.3 16.4 %copy-start.26 = (f32[768]{0:T(1024)}, f32[768]{0:T(1024)S(1)}, u32[]{:S(2)}) copy-start(f32[768]{0:T(1024)S(1)} %convert_element_type.164) | copy-start | bytes 9220
  36.9 6.0 copy-start
  42.9 1.7 copy-start.30
  44.7 3.5 copy-start.23
  48.2 5.1 copy-start.19
  55.9 1.2 copy-start.29
  99.2 8.3 %copy-start.9 = (bf16[8,512,3,64]{1,3,2,0:T(8,128)(2,1)}, bf16[8,512,3,64]{1,3,2,0:T(8,128)(2,1)S(1)}, u32[]{:S(2)}) copy-start(bf16[8,512,3,64]{1,3,2,0:T(8,128)(2,1)S(1)} %get-tuple-element.505) | copy-start | bytes 4718596
  99.2 8.3 %copy-start.10 = (bf16[8,512,3,64]{1,3,2,0:T(8,128)(2,1)}, bf16[8,512,3,64]{1,3,2,0:T(8,128)(2,1)S(1)}, u32[]{:S(2)}) copy-start(bf16[8,512,3,64]{1,3,2,0:T(8,128)(2,1)S(1)} %get-tuple-element.506) | copy-start | bytes 4718596
  99.2 8.3 %copy-start.28 = (s32[8,512]{1,0:T(8,128)}, s32[8,512]{1,0:T(8,128)S(1)}, u32[]{:S(2)}) copy-start(s32[8,512]{1,0:T(8,128)S(1)} %get-tuple-element.531) | copy-start | bytes 49156
  110.5 32.2 %all-to-all-start = ((bf16[4,1024,192]{1,2,0:T(8,128)(2,1)}), bf16[4,1024,192]{1,2,0:T(8,128)(2,1)S(1)}, u32[]{:S(2)}, u32[]{:S(2)}) async-start(bf16[4,1024,192]{1,2,0:T(8,128)(2,1)} %copy.85), calls=%async_computation | async-start | bytes 3145728 | tf_op jit(solution)/shard_map/all_to_all | solution.py:169
  114.1 72.2 %all-gather.9.cloned.1.call-start = ((), (), s32[]{:S(2)}) async-start(), calls=%async_computation.8 | async-start | bytes 5898240 | tf_op jit(solution)/shard_map/all_gather | solution.py:150
  114.8 9.3 %copy-start.31 = (bf16[768]{0:T(1024)(128)(2,1)S(1)}, bf16[768]{0:T(1024)(128)(2,1)}, u32[]{:S(2)}) copy-start(bf16[768]{0:T(1024)(128)(2,1)} %param.30) | copy-start | bytes 4612
  114.8 26.2 %copy-start.17 = (bf16[1024,768]{1,0:T(8,128)(2,1)S(1)}, bf16[1024,768]{1,0:T(8,128)(2,1)}, u32[]{:S(2)}) copy-start(bf16[1024,768]{1,0:T(8,128)(2,1)} %param.33) | copy-start | bytes 4718596
  114.8 328.0 %reduce-scatter.7.cloned.1.call-start = ((), (), s32[]{:S(2)}) async-start(), calls=%async_computation.11 | async-start | bytes 1474560 | tf_op jit(solution)/shard_map/reduce_scatter | solution.py:256
  142.7 1.1 copy-start.20
  218.2 2.9 copy-start.1
  221.2 1.4 copy-start.5
  222.0 1.7 copy-start.2
  222.6 2.3 copy-start.21
  223.7 1.1 copy-start.22
  227.4 215.5 %reduce-scatter.9.cloned.1.call-start = ((), (), s32[]{:S(2)}) async-start(), calls=%async_computation.12 | async-start | bytes 5898240 | tf_op jit(solution)/shard_map/reduce_scatter | solution.py:259
  241.6 27.9 %all-to-all-start.1 = ((bf16[1024,4,192]{0,2,1:T(8,128)(2,1)}), bf16[1024,4,192]{0,2,1:T(8,128)(2,1)}, u32[]{:S(2)}, u32[]{:S(2)}) async-start(bf16[1024,4,192]{0,2,1:T(8,128)(2,1)} %bitcast.218), calls=%async_computation.1 | async-start | bytes 3145728 | tf_op jit(solution)/shard_map/all_to_all | solution.py:190
  246.1 196.8 %reduce-scatter.11.cloned.1.call-start = ((), (), s32[]{:S(2)}) async-start(), calls=%async_computation.13 | async-start | bytes 5898240 | tf_op jit(solution)/shard_map/reduce_scatter | solution.py:262
  255.3 221.0 %reduce-scatter.5.cloned.1.call-start = ((), (), s32[]{:S(2)}) async-start(), calls=%async_computation.9 | async-start | bytes 7864320 | tf_op jit(solution)/shard_map/reduce_scatter | solution.py:216
  386.7 3.1 copy-start.18
  389.8 16.3 %copy-start.16 = (bf16[24,8,8,512]{3,1,2,0:T(8,128)(2,1)}, bf16[24,8,8,512]{3,1,2,0:T(8,128)(2,1)S(1)}, u32[]{:S(2)}) copy-start(bf16[24,8,8,512]{3,1,2,0:T(8,128)(2,1)S(1)} %copy.116) | copy-start | bytes 4718596
  389.8 2.0 copy-start.7
  391.4 2.0 copy-start.12
  391.8 1.6 copy-start.24
  393.3 6.5 copy-start.14
  418.3 3.1 copy-start.32
  418.3 319.9 %all-reduce.19.cloned.1.call-start = ((), (), s32[]{:S(2)}) async-start(), calls=%async_computation.10 | async-start | bytes 3538944 | tf_op jit(solution)/shard_map/psum | solution.py:266
  422.0 3.0 copy-start.8
  427.1 6.8 copy-start.13
  427.1 12.0 %slice-start = ((s8[6291456]{0:T(1024)(128)(4,1)}), s8[4194304]{0:T(1024)(128)(4,1)S(1)}, s32[]{:S(2)}) async-start(s8[6291456]{0:T(1024)(128)(4,1)} %bitcast.214), calls=%async_computation.14 | async-start | bytes 8388608
  434.0 5.2 copy-start.15
  434.0 5.2 slice-start.1
  441.4 34.9 %copy-start.27 = (f32[768]{0:T(1024)S(1)}, f32[768]{0:T(1024)}, u32[]{:S(2)}) copy-start(f32[768]{0:T(1024)} %copy-done.26) | copy-start | bytes 9220
  476.3 3.3 copy-start.4
  479.5 3.7 copy-start.3
  479.5 3.7 copy-start.6
  511.0 2.7 copy-start.11
  513.7 2.7 copy-start.25
Sparse Core Ops, SparseCore 0:
  9.5 20.3 all-gather.4
  31.5 37.4 all-gather.6
  116.4 44.5 all-gather.8
  227.5 29.6 reduce-scatter.6
  259.6 47.4 reduce-scatter.8
  309.5 47.9 reduce-scatter.10
  418.4 57.8 reduce-scatter.4
  480.4 120.0 all-reduce.18
where the time goes:
time: 760 us; the launch traced here: 748 us
  blocking collectives  263 us (35%)
  matrix products  259 us (34%)
  local copies, waits for them, and re-layouts  77.2 us (10%)
  other arithmetic  73.1 us (10%)
  waiting for transfers between devices  49.9 us (7%)
  between operations  16.9 us (2%)
  starting transfers between devices  8.29 us (1%)
    psum x1, blocking collectives, per_device(): lax.psum((share_gain_one, share_shift_one, grad_qkvw, grad_bias_qv, share...  222 us
    dot_general x6, matrix products, against(): lax.dot_general(left, right, (((1,), (1,)), ((), ())), preferred_element_...  57.6 us
    dot_general x6, matrix products, plain_dot(): return jnp.dot(left, right, preferred_element_type=jnp.float32)  55.7 us
    dot_general x6, matrix products, over_rows(): lax.dot_general(left, right, (((0,), (0,)), ((), ())), preferred_element_...  35.7 us
    unnamed x95, local copies, waits for them, and re-layouts  33.9 us
    reduce_scatter x1, waiting for transfers between devices, per_device(): lax.psum_scatter(partial_normed.astype(jnp.bfloat16), 'mp', scatter_dimen...  33.4 us
    unnamed x2, blocking collectives  24.6 us
    dot_general x16, matrix products, head_scores(): jnp.einsum('qhd,khd->hqk', query_heads, key_heads, preferred_element_type...  23.6 us
  transfers between devices with their start and end apart: 10, of which 2 were waited for; matrix products, arithmetic and copies ran while one was open for 48% of the time, Pallas kernels for 0%

commit v1 on v0

--- a/solution.py
+++ b/solution.py
@@ -187,12 +187,18 @@
     grad_bias_out = jnp.sum(grad_hidden, axis=0)
     grad_proj = grad_hidden.astype(jnp.bfloat16)
     grad_outw = over_rows(attended_rows, grad_proj)
-    grad_attended = lax.all_to_all(
-        against(grad_proj, full_out).astype(jnp.bfloat16),
-        "mp",
-        split_axis=1,
-        concat_axis=0,
-        tiled=True,
+    grad_attended = jnp.concatenate(
+        lax.all_to_all(
+            jnp.stack(
+                jnp.split(
+                    against(grad_proj, full_out).astype(jnp.bfloat16), lax.axis_size("mp"), axis=1
+                )
+            ),
+            "mp",
+            0,
+            0,
+        ),
+        axis=0,
     )
     grad_query, grad_key, grad_value = lax.map(
         attend_backward,

time: 760 us -> 760 us (level)
  no operation moved by 1% of the time
where the time goes in v1:
time: 760 us; the launch traced here: 748 us
  blocking collectives  263 us (35%)
  matrix products  257 us (34%)
  local copies, waits for them, and re-layouts  77.6 us (10%)
  other arithmetic  74.8 us (10%)
  waiting for transfers between devices  49.4 us (6%)
  between operations  16.9 us (2%)
  starting transfers between devices  8.25 us (1%)
    psum x1, blocking collectives, per_device(): lax.psum((share_gain_one, share_shift_one, grad_qkvw, grad_bias_qv, share...  222 us
    dot_general x6, matrix products, against(): lax.dot_general(left, right, (((1,), (1,)), ((), ())), preferred_element_...  56.5 us
    dot_general x6, matrix products, plain_dot(): return jnp.dot(left, right, preferred_element_type=jnp.float32)  55.7 us
    dot_general x6, matrix products, over_rows(): lax.dot_general(left, right, (((0,), (0,)), ((), ())), preferred_element_...  35.5 us
    unnamed x95, local copies, waits for them, and re-layouts  33.9 us
    reduce_scatter x1, waiting for transfers between devices, per_device(): lax.psum_scatter(partial_normed.astype(jnp.bfloat16), 'mp', scatter_dimen...  33.2 us
    unnamed x2, blocking collectives  24.6 us
    dot_general x16, matrix products, head_scores(): jnp.einsum('qhd,khd->hqk', query_heads, key_heads, preferred_element_type...  23.6 us
  transfers between devices with their start and end apart: 10, of which 2 were waited for; matrix products, arithmetic and copies ran while one was open for 48% of the time, Pallas kernels for 0%

profile of v1, /device:TPU:0, one launch (start us, length us, event | category | flops | bytes accessed | tf_op | source)
XLA Modules:
  0.0 747.9 jit_solution(5415918857712550685)
XLA Ops:
  14.9 13.4 %all-reduce.15 = (bf16[768]{0:T(1024)(128)(2,1)S(1)}, bf16[768]{0:T(1024)(128)(2,1)S(1)}, bf16[768]{0:T(1024)(128)(2,1)S(1)}, bf16[768]{0:T(1024)(128)(2,1)S(1)}, bf16[768]{0:T(1024)(128)(2,1)S(1)}) all-reduce(bf16[768]{0:T(1024)(128)(2,1)S(1)} %dynamic-update-slice.1, ...), channel_id=1, replica_groups=mesh['dp'=8,'mp'=4] {'mp'}, use_global_device_ids=true, to_apply=%add.1 | all-reduce | flops 3840 | bytes 15360
  28.3 8.6 %copy.80 = bf16[4096,768]{0,1:T(8,128)(2,1)} copy(bf16[4096,768]{1,0:T(8,128)(2,1)} %param.19) | data formatting | bytes 12582912 | tf_op args[0]
  36.9 4.7 convert_reduce_fusion
  44.7 3.5 add_convert_fusion.2
  58.4 40.7 %while.26 = (s32[]{:T(128)}, bf16[8,512,3,64]{1,3,2,0:T(8,128)(2,1)}, f32[8,3,512]{2,1,0:T(4,128)}, bf16[8,512,3,64]{1,3,2,0:T(8,128)(2,1)}, s32[8,512]{1,0:T(8,...) while((s32[]{:T(128)}, ...), condition=%wide.region_5.6_spmd, body=%wide.region_2.5_spmd.sunk | while | flops 211909632 | bytes 11333209 | solution.py:166
  61.0 2.7 fusion.146
  66.0 2.7 fusion.146
  71.1 2.7 fusion.146
  76.2 2.7 fusion.146
  81.3 2.7 fusion.146
  86.3 2.7 fusion.146
  91.4 2.7 fusion.146
  96.5 2.7 fusion.146
  99.2 4.6 copy.84
  103.7 3.7 all_to_all.17
  107.5 3.0 copy.85
  110.5 3.6 all-to-all-start
  114.9 9.2 %convert_element_type.163 = f32[4096,768]{0,1:T(8,128)} convert(bf16[4096,768]{0,1:T(8,128)(2,1)} %copy.80) | non-fusion elementwise | flops 3145728 | bytes 18874368 | tf_op jit(solution)/shard_map/convert_element_type | solution.py:156
  124.1 16.9 %all-gather = bf16[4,1,768]{2,1,0:T(2,128)(2,1)S(1)} all-gather(bf16[1,1,768]{2,1,0:T(2,128)(2,1)S(1)} %reshape.302), channel_id=1, replica_groups=mesh['dp'=8,'mp'=4] {'mp'}, dimensions={0}, use_global_device_ids=true | all-gather | bytes 7680 | tf_op jit(solution)/shard_map/all_gather | solution.py:147
  143.8 4.3 fusion.91
  148.5 37.7 %multiply_convert_fusion.1 = (bf16[1024,3072]{1,0:T(8,128)(2,1)}, f32[1024,3072]{1,0:T(8,128)}, f32[1024,3072]{1,0:T(8,128)}) fusion(f32[3072]{0:T(1024)S(1)} %bitcast.229, bf16[768,3072]{1,0:T(8,128)(2,1)} %all-gather.7.cloned.1.call-done, f32[1024,768]{0,1:T(8,128)S(1)} %get-tuple-element.293, f32[768]{0:T(1024)S(1)} %convert_element_type.172, ...), kind=kOutput, calls=%fused_computation.70 | convolution fusion | flops 5043388416 | bytes 39348224 | tf_op jit(solution)/shard_map/dot_general | solution.py:31
  186.2 18.7 %fusion.93 = (bf16[3072]{0:T(1024)(128)(2,1)S(1)}, bf16[1024,3072]{1,0:T(8,128)(2,1)}) fusion(f32[1024,3072]{1,0:T(8,128)} %get-tuple-element.275, bf16[1024,768]{1,0:T(8,128)(2,1)} %param.33, bf16[3072,768]{1,0:T(8,128)(2,1)} %all-gather.9.cloned.1.call-done, f32[1024,3072]{1,0:T(8,128)} %get-tuple-element.294, f32[3072]{0:T(1024)S(1)} %bitcast.230), kind=kOutput, calls=%fused_computation.170 | convolution fusion | flops 4882166784 | bytes 37767168 | tf_op jit(solution)/shard_map/dot_general | solution.py:41
  204.9 9.8 %fusion.92 = (bf16[768]{0:T(1024)(128)(2,1)S(1)}, f32[1024,768]{1,0:T(8,128)}) fusion(bf16[1024,3072]{1,0:T(8,128)(2,1)} %get-tuple-element.298, bf16[768,3072]{1,0:T(8,128)(2,1)} %all-gather.7.cloned.1.call-done), kind=kOutput, calls=%fused_computation.169 | convolution fusion | flops 4832623616 | bytes 14157312 | tf_op jit(solution)/shard_map/dot_general | solution.py:41
  214.7 3.6 copy.88
  218.2 2.9 multiply_reduce_fusion.2
  224.9 2.5 convolution_convert_fusion.4
  227.4 9.9 %convolution_convert_fusion.1 = bf16[768,3072]{1,0:T(8,128)(2,1)} fusion(bf16[1024,3072]{1,0:T(8,128)(2,1)} %get-tuple-element.298, f32[1024,768]{0,1:T(8,128)S(1)} %get-tuple-element.293, f32[768]{0:T(1024)S(1)} %convert_element_type.172, f32[768]{0:T(1024)S(1)} %convert_element_type.171, f32[1024]{0:T(1024)S(1)} %fusion.85, ...), kind=kOutput, calls=%fused_computation.88 | convolution fusion | flops 4838129664 | bytes 14170112 | tf_op jit(solution)/shard_map/dot_general | solution.py:35
  237.3 3.2 convolution_convert_fusion.3
  242.0 4.4 all-to-all-start.1
  246.4 9.1 %convolution_convert_fusion = bf16[3072,768]{1,0:T(8,128)(2,1)} fusion(bf16[1024,3072]{1,0:T(8,128)(2,1)} %get-tuple-element.274, bf16[1024,768]{1,0:T(8,128)(2,1)} %param.33), kind=kOutput, calls=%fused_computation.87 | convolution fusion | flops 4834197504 | bytes 12582912 | tf_op jit(solution)/shard_map/dot_general | solution.py:35
  255.6 14.0 %all-to-all-done.1 = bf16[4,1024,192]{1,2,0:T(8,128)(2,1)} async-done(((bf16[4,1024,192]{1,2,0:T(8,128)(2,1)}), bf16[4,1024,192]{1,2,0:T(8,128)(2,1)}, u32[]{:S(2)}, u32[]{:S(2)}) %all-to-all-start.1) | async-done | bytes 1572896 | tf_op jit(solution)/shard_map/all_to_all | solution.py:191
  269.6 3.9 copy.89
  273.4 3.5 reshape_reshape.3
  276.9 3.4 copy.92
  284.3 102.6 %while.27 = (s32[]{:T(128)}, bf16[8,512,3,64]{1,3,2,0:T(8,128)(2,1)}, bf16[8,512,3,64]{1,3,2,0:T(8,128)(2,1)}, bf16[8,512,3,64]{1,3,2,0:T(8,128)(2,1)}, bf16[8,5...) while((s32[]{:T(128)}, ...), condition=%wide.region_12.13_spmd, body=%wide.region_10.12_spmd.sunk | while | flops 511933440 | bytes 26126452 | solution.py:203
  290.7 2.2 fusion.158
  294.9 2.2 fusion.159
  303.5 2.2 fusion.158
  316.3 2.2 fusion.158
  320.6 2.2 fusion.159
  329.2 2.2 fusion.158
  342.0 2.2 fusion.158
  346.2 2.2 fusion.159
  354.8 2.2 fusion.158
  367.6 2.2 fusion.158
  380.3 2.2 fusion.158
  386.9 2.4 copy.98
  393.6 6.4 fusion.71
  400.0 6.3 fusion.74
  406.3 12.1 %add_convert_fusion = bf16[4096,768]{0,1:T(8,128)(2,1)} fusion(f32[4096,768]{0,1:T(8,128)} %fusion.74, f32[4096,768]{0,1:T(8,128)} %fusion.71, bf16[4096,192]{0,1:T(8,128)(2,1)S(1)} %bitcast.212, bf16[3,768,192]{1,2,0:T(8,128)(2,1)S(1)} %copy-done.24), kind=kOutput, calls=%fused_computation.68 | convolution fusion | flops 1217396736 | bytes 33325056 | tf_op jit(solution)/shard_map/dot_general | solution.py:41
  422.2 2.8 dynamic-slice_reduce_fusion
  427.6 6.6 convolution_bitcast_fusion
  434.2 5.2 convolution_bitcast_fusion.1
  439.4 2.2 convolution_bitcast_fusion.2
  443.1 33.2 %reduce-scatter.5.cloned.1.call-done = bf16[1024,768]{0,1:T(8,128)(2,1)} async-done(((bf16[4096,768]{0,1:T(8,128)(2,1)}), bf16[1024,768]{0,1:T(8,128)(2,1)}) %reduce-scatter.5.cloned.1.call-update) | async-done | bytes 1572880 | tf_op jit(solution)/shard_map/reduce_scatter | solution.py:222
  476.3 3.2 multiply_reduce_fusion.3
  479.6 3.6 fusion.67
  483.2 5.3 add_add_fusion.2
  490.2 11.2 %all-reduce.14 = (bf16[768]{0:T(1024)(128)(2,1)S(1)}, bf16[768]{0:T(1024)(128)(2,1)S(1)}, bf16[768]{0:T(1024)(128)(2,1)S(1)}, bf16[768]{0:T(1024)(128)(2,1)S(1)}...) all-reduce(bf16[768]{0:T(1024)(128)(2,1)S(1)} %dynamic-update-slice, ...), channel_id=1, replica_groups=mesh['dp'=8,'mp'=4] {'mp'}, use_global_device_ids=true, to_apply=%add.5 | all-reduce | flops 8448 | bytes 33792
  501.4 9.5 %add_convert_fusion.3 = bf16[1024,768]{0,1:T(8,128)(2,1)} fusion(f32[1024,768]{0,1:T(8,128)S(1)} %get-tuple-element.293, bf16[1024,3072]{1,0:T(8,128)(2,1)} %get-tuple-element.274, bf16[3072,768]{1,0:T(8,128)(2,1)} %all-gather.9.cloned.1.call-done, f32[768]{0:T(1024)S(1)} %convert_element_type.176), kind=kOutput, calls=%fused_computation.109 | convolution fusion | flops 4834197504 | bytes 15731712 | tf_op jit(solution)/shard_map/dot_general | solution.py:31
  511.0 2.7 copy.101
  513.7 2.4 copy.102
  516.4 221.7 %all-reduce.20 = (f32[192]{0:T(256)}, f32[192]{0:T(256)}, f32[2,192]{1,0:T(2,128)}, f32[192,768]{1,0:T(8,128)}, f32[192]{0:T(256)}, /*index=5*/f32[192]{0:T(256)...) all-reduce(f32[192]{0:T(256)S(1)} %get-tuple-element.306, ...), channel_id=1, replica_groups=mesh['dp'=8,'mp'=4] {'dp'}, use_global_device_ids=true, to_apply=%region_20.21 | all-reduce | flops 1329408 | bytes 7981056 | tf_op jit(solution)/shard_map/psum | solution.py:272
  738.1 2.8 copy.168
  (265 shorter events, 143.0 us)
Async XLA Ops:
  7.2 135.5 %all-gather.5.cloned.1.call-start = ((), (), s32[]{:S(2)}) async-start(), calls=%async_computation.6 | async-start | bytes 1474560 | tf_op jit(solution)/shard_map/all_gather | solution.py:148
  7.9 140.6 %all-gather.7.cloned.1.call-start = ((), (), s32[]{:S(2)}) async-start(), calls=%async_computation.7 | async-start | bytes 5898240 | tf_op jit(solution)/shard_map/all_gather | solution.py:149
  28.3 16.4 %copy-start.26 = (f32[768]{0:T(1024)}, f32[768]{0:T(1024)S(1)}, u32[]{:S(2)}) copy-start(f32[768]{0:T(1024)S(1)} %convert_element_type.164) | copy-start | bytes 9220
  36.9 6.0 copy-start
  42.9 1.7 copy-start.30
  44.7 3.5 copy-start.23
  48.2 5.1 copy-start.19
  55.9 1.2 copy-start.29
  99.2 8.3 %copy-start.9 = (bf16[8,512,3,64]{1,3,2,0:T(8,128)(2,1)}, bf16[8,512,3,64]{1,3,2,0:T(8,128)(2,1)S(1)}, u32[]{:S(2)}) copy-start(bf16[8,512,3,64]{1,3,2,0:T(8,128)(2,1)S(1)} %get-tuple-element.509) | copy-start | bytes 4718596
  99.2 8.3 %copy-start.10 = (bf16[8,512,3,64]{1,3,2,0:T(8,128)(2,1)}, bf16[8,512,3,64]{1,3,2,0:T(8,128)(2,1)S(1)}, u32[]{:S(2)}) copy-start(bf16[8,512,3,64]{1,3,2,0:T(8,128)(2,1)S(1)} %get-tuple-element.510) | copy-start | bytes 4718596
  99.2 8.3 %copy-start.28 = (s32[8,512]{1,0:T(8,128)}, s32[8,512]{1,0:T(8,128)S(1)}, u32[]{:S(2)}) copy-start(s32[8,512]{1,0:T(8,128)S(1)} %get-tuple-element.535) | copy-start | bytes 49156
  110.5 32.2 %all-to-all-start = ((bf16[4,1024,192]{1,2,0:T(8,128)(2,1)}), bf16[4,1024,192]{1,2,0:T(8,128)(2,1)S(1)}, u32[]{:S(2)}, u32[]{:S(2)}) async-start(bf16[4,1024,192]{1,2,0:T(8,128)(2,1)} %copy.85), calls=%async_computation | async-start | bytes 3145728 | tf_op jit(solution)/shard_map/all_to_all | solution.py:169
  114.1 72.2 %all-gather.9.cloned.1.call-start = ((), (), s32[]{:S(2)}) async-start(), calls=%async_computation.8 | async-start | bytes 5898240 | tf_op jit(solution)/shard_map/all_gather | solution.py:150
  114.8 9.3 %copy-start.31 = (bf16[768]{0:T(1024)(128)(2,1)S(1)}, bf16[768]{0:T(1024)(128)(2,1)}, u32[]{:S(2)}) copy-start(bf16[768]{0:T(1024)(128)(2,1)} %param.30) | copy-start | bytes 4612
  114.8 26.2 %copy-start.17 = (bf16[1024,768]{1,0:T(8,128)(2,1)S(1)}, bf16[1024,768]{1,0:T(8,128)(2,1)}, u32[]{:S(2)}) copy-start(bf16[1024,768]{1,0:T(8,128)(2,1)} %param.33) | copy-start | bytes 4718596
  114.8 328.2 %reduce-scatter.7.cloned.1.call-start = ((), (), s32[]{:S(2)}) async-start(), calls=%async_computation.11 | async-start | bytes 1474560 | tf_op jit(solution)/shard_map/reduce_scatter | solution.py:262
  142.7 1.1 copy-start.20
  218.2 2.9 copy-start.1
  221.2 1.4 copy-start.5
  222.0 1.7 copy-start.2
  222.6 2.3 copy-start.21
  223.7 1.1 copy-start.22
  227.4 215.7 %reduce-scatter.9.cloned.1.call-start = ((), (), s32[]{:S(2)}) async-start(), calls=%async_computation.12 | async-start | bytes 5898240 | tf_op jit(solution)/shard_map/reduce_scatter | solution.py:265
  242.0 27.6 %all-to-all-start.1 = ((bf16[4,1024,192]{1,2,0:T(8,128)(2,1)}), bf16[4,1024,192]{1,2,0:T(8,128)(2,1)}, u32[]{:S(2)}, u32[]{:S(2)}) async-start(bf16[4,1024,192]{1,2,0:T(8,128)(2,1)} %pad_maximum_fusion.1), calls=%async_computation.1 | async-start | bytes 3145728 | tf_op jit(solution)/shard_map/all_to_all | solution.py:191
  246.3 196.7 %reduce-scatter.11.cloned.1.call-start = ((), (), s32[]{:S(2)}) async-start(), calls=%async_computation.13 | async-start | bytes 5898240 | tf_op jit(solution)/shard_map/reduce_scatter | solution.py:268
  255.6 220.7 %reduce-scatter.5.cloned.1.call-start = ((), (), s32[]{:S(2)}) async-start(), calls=%async_computation.9 | async-start | bytes 7864320 | tf_op jit(solution)/shard_map/reduce_scatter | solution.py:222
  386.9 3.1 copy-start.18
  390.0 16.3 %copy-start.16 = (bf16[24,8,8,512]{3,1,2,0:T(8,128)(2,1)}, bf16[24,8,8,512]{3,1,2,0:T(8,128)(2,1)S(1)}, u32[]{:S(2)}) copy-start(bf16[24,8,8,512]{3,1,2,0:T(8,128)(2,1)S(1)} %copy.116) | copy-start | bytes 4718596
  390.0 2.0 copy-start.7
  391.6 2.0 copy-start.12
  392.0 1.6 copy-start.24
  393.5 6.5 copy-start.14
  418.5 3.1 copy-start.32
  418.5 319.6 %all-reduce.19.cloned.1.call-start = ((), (), s32[]{:S(2)}) async-start(), calls=%async_computation.10 | async-start | bytes 3538944 | tf_op jit(solution)/shard_map/psum | solution.py:272
  422.2 3.3 copy-start.8
  427.6 6.6 copy-start.13
  427.6 11.8 %slice-start = ((s8[6291456]{0:T(1024)(128)(4,1)}), s8[4194304]{0:T(1024)(128)(4,1)S(1)}, s32[]{:S(2)}) async-start(s8[6291456]{0:T(1024)(128)(4,1)} %bitcast.220), calls=%async_computation.14 | async-start | bytes 8388608
  434.2 5.2 copy-start.15
  434.2 5.2 slice-start.1
  441.6 34.7 %copy-start.27 = (f32[768]{0:T(1024)S(1)}, f32[768]{0:T(1024)}, u32[]{:S(2)}) copy-start(f32[768]{0:T(1024)} %copy-done.26) | copy-start | bytes 9220
  476.3 3.3 copy-start.4
  479.5 3.7 copy-start.3
  479.5 3.7 copy-start.6
  511.0 2.7 copy-start.11
  513.7 2.7 copy-start.25
Sparse Core Ops, SparseCore 0:
  9.5 20.3 all-gather.4
  31.5 37.4 all-gather.6
  116.4 44.5 all-gather.8
  227.5 29.3 reduce-scatter.6
  259.3 47.5 reduce-scatter.8
  309.2 47.9 reduce-scatter.10
  418.6 57.6 reduce-scatter.4
  480.4 120.1 all-reduce.18
